TPU v7x, 32 devices: a whole 2x2x4 slice. The times are simulated.
32 devices in a mesh: mp: 4 (over y, core), latent: 8 (over z, x).
Axes of the slice: x: 2, y: 2, z: 4, core: 2. Of those that a mesh axis runs over, the one named last changes fastest.
Arguments:
- resid_clean: bfloat16 [128, 4608], P(('mp', 'latent')), may hold values from -6 to 6
- resid_corrupt: bfloat16 [128, 4608], P(('mp', 'latent')), may hold values from -6 to 6
- answer_ids: int32 [128, 2], replicated, may hold values from 0 to 127, all different within a row
- unembed: bfloat16 [128, 4608], replicated, may hold values from -1.5 to 1.5
- pre_gain: float32 [4608], replicated, may hold values from 0.25 to 1.75
- post_gain: float32 [4608], replicated, may hold values from 0.25 to 1.75
- final_gain: float32 [4608], replicated, may hold values from 0.25 to 1.75
- w_gate: bfloat16 [4608, 36864], P(None, ('mp', 'latent')), may hold values from -0.09375 to 0.09375
- w_up: bfloat16 [4608, 36864], P(None, ('mp', 'latent')), may hold values from -0.09375 to 0.09375
- w_down: bfloat16 [36864, 4608], P(('mp', 'latent')), may hold values from -0.03125 to 0.03125
- w_enc: bfloat16 [4608, 65536], P(None, ('mp', 'latent')), may hold values from -0.09375 to 0.09375
- b_enc: float32 [65536], P(('mp', 'latent')), may hold values from -3 to 3
- w_dec: bfloat16 [65536, 4608], P(('mp', 'latent')), may hold values from -0.09375 to 0.09375
Outputs:
- attribution: float32 [1, 65536], P(None, ('mp', 'latent'))
Inputs may be any that keep to these rules, and one draw needn't show every extreme that they name: `answer_ids`: the two indices of a token differ.
All inputs are finite; a program needn't handle non-finite values.
Results may differ from a plain program's by a relative error of at most 0.0056.
Values may be sent and summed in bfloat16 or wider, within the bound.
A program may use at most 128 MiB of HBM per device.

v0:
```python
import jax
import jax.numpy as jnp
from jax import lax
from jax.sharding import PartitionSpec as P

SEQ = 128


epsilon = 1e-06
gelu_scale = 0.7978845608028654
gelu_cubic = 0.044715


def gelu_tanh(value):
    return 0.5 * value * (1.0 + jnp.tanh(gelu_scale * (value + gelu_cubic * value * value * value)))


def gelu_slope(value):
    inner = jnp.tanh(gelu_scale * (value + gelu_cubic * value * value * value))
    return 0.5 * (1.0 + inner) + 0.5 * value * (1.0 - inner * inner) * gelu_scale * (
        1.0 + 3.0 * gelu_cubic * value * value
    )


def contract_last(left, right):
    return lax.dot_general(
        left, right, (((1,), (1,)), ((), ())), preferred_element_type=jnp.float32
    )


def output_grads(stream, mlp_out, answers, unembed, post_gain, final_gain):
    inv_post = lax.rsqrt(jnp.mean(mlp_out * mlp_out, axis=-1, keepdims=True) + epsilon)
    output = stream + mlp_out * inv_post * post_gain
    inv_final = lax.rsqrt(jnp.mean(output * output, axis=-1, keepdims=True) + epsilon)
    candidate = lax.broadcasted_iota(jnp.int32, (answers.shape[0], unembed.shape[0]), 1)
    selector = (
        (candidate == answers[:, 0:1]).astype(jnp.float32)
        - (candidate == answers[:, 1:2]).astype(jnp.float32)
    ).astype(jnp.bfloat16)
    direction = jnp.dot(selector, unembed, preferred_element_type=jnp.float32)
    weighted = final_gain * direction
    grad_output = inv_final * weighted - output * (inv_final * inv_final * inv_final) * jnp.mean(
        weighted * output, axis=-1, keepdims=True
    )
    post_grad = post_gain * grad_output
    grad_mlp = (
        inv_post * post_grad
        - mlp_out
        * (inv_post * inv_post * inv_post)
        * jnp.mean(post_grad * mlp_out, axis=-1, keepdims=True)
    ).astype(jnp.bfloat16)
    return (grad_output, grad_mlp)


def local(
    resid_clean,
    resid_corrupt,
    answer_ids,
    unembed,
    pre_gain,
    post_gain,
    final_gain,
    w_gate,
    w_up,
    w_down,
    w_enc,
    b_enc,
    w_dec,
):
    own_rows = resid_clean.shape[0]
    clean_all, corrupt_all = (
        lax.all_gather(resid_clean, ("mp", "latent"), axis=0, tiled=True),
        lax.all_gather(resid_corrupt, ("mp", "latent"), axis=0, tiled=True),
    )
    total_rows = clean_all.shape[0]
    offset = lax.axis_index(("mp", "latent")) * own_rows
    stream = clean_all.astype(jnp.float32)
    inv_pre = lax.rsqrt(jnp.mean(stream * stream, axis=-1, keepdims=True) + epsilon)
    normed = (stream * inv_pre * pre_gain).astype(jnp.bfloat16)
    gate_pre = jnp.dot(normed, w_gate, preferred_element_type=jnp.float32)
    up_proj = jnp.dot(normed, w_up, preferred_element_type=jnp.float32)
    activated = gelu_tanh(gate_pre)
    hidden = (activated * up_proj).astype(jnp.bfloat16)
    stream_rows = lax.dynamic_slice_in_dim(stream, offset, own_rows, 0)
    inv_rows = lax.dynamic_slice_in_dim(inv_pre, offset, own_rows, 0)
    mlp_out = lax.psum(
        jnp.dot(hidden, w_down, preferred_element_type=jnp.float32), ("mp", "latent")
    )
    grad_output, grad_mlp = output_grads(
        stream, mlp_out, answer_ids, unembed, post_gain, final_gain
    )
    grad_hidden = contract_last(grad_mlp, w_down)
    grad_rows_out = lax.dynamic_slice_in_dim(grad_output, offset, own_rows, 0)
    grad_gate = (grad_hidden * up_proj * gelu_slope(gate_pre)).astype(jnp.bfloat16)
    grad_up = (grad_hidden * activated).astype(jnp.bfloat16)
    grad_normed = lax.psum_scatter(
        contract_last(grad_gate, w_gate) + contract_last(grad_up, w_up),
        ("mp", "latent"),
        scatter_dimension=0,
        tiled=True,
    )
    pre_grad = pre_gain * grad_normed
    grad_stream = (
        grad_rows_out
        + inv_rows * pre_grad
        - stream_rows
        * (inv_rows * inv_rows * inv_rows)
        * jnp.mean(pre_grad * stream_rows, axis=-1, keepdims=True)
    ).astype(jnp.bfloat16)
    clean_code = jax.nn.relu(jnp.dot(clean_all, w_enc, preferred_element_type=jnp.float32) + b_enc)
    corrupt_code = jax.nn.relu(
        jnp.dot(corrupt_all, w_enc, preferred_element_type=jnp.float32) + b_enc
    )
    change = clean_code - corrupt_code
    projected = contract_last(
        lax.all_gather(grad_stream, ("mp", "latent"), axis=0, tiled=True), w_dec
    )
    product = change * projected
    return jnp.sum(product.reshape(total_rows // SEQ, SEQ, product.shape[1]), axis=1)


def solution(mesh):
    return jax.shard_map(
        local,
        mesh=mesh,
        in_specs=(
            P(("mp", "latent"), None),
            P(("mp", "latent"), None),
            P(),
            P(),
            P(),
            P(),
            P(),
            P(None, ("mp", "latent")),
            P(None, ("mp", "latent")),
            P(("mp", "latent"), None),
            P(None, ("mp", "latent")),
            P(("mp", "latent")),
            P(("mp", "latent"), None),
        ),
        out_specs=P(None, ("mp", "latent")),
        check_vma=False,
    )
```

profile of v0, /device:TPU:0, one launch (start us, length us, event | category | flops | bytes accessed | tf_op | source)
XLA Modules:
  0.0 512.9 jit_solution(18064618967824997244)
XLA Ops:
  6.5 0.7 all-gather.7.cloned.1.call-update
  7.3 59.9 %all-gather.7.cloned.1.call-done = bf16[32,4,4608]{2,1,0:T(4,128)(2,1)} async-done(((bf16[1,4,4608]{2,1,0:T(4,128)(2,1)}), bf16[32,4,4608]{2,1,0:T(4,128)(2,1)}) %all-gather.7.cloned.1.call-update) | async-done | bytes 1179664 | tf_op jit(solution)/shard_map/all_gather | solution.py:72
  67.2 1.4 reshape.70
  68.6 0.3 multiply_reduce_fusion.4
  69.0 6.0 %fusion.17 = f32[128,1152]{1,0:T(8,128)S(1)} fusion(bf16[4608,1152]{1,0:T(8,128)(2,1)} %param.20, bf16[128,4608]{1,0:T(8,128)(2,1)S(1)} %reshape.70, f32[4608]{0:T(1024)S(1)} %copy-done.3, f32[128]{0:T(128)S(1)} %add_rsqrt_fusion.2), kind=kOutput, calls=%fused_computation.36 | convolution fusion | flops 1361313792 | bytes 12405248 | tf_op jit(solution)/shard_map/dot_general | solution.py:80
  75.2 0.6 slice-done.5
  75.8 1.7 fusion.16
  77.6 0.6 slice-done.7
  78.2 0.8 slice-done.8
  79.0 3.2 fusion.18
  82.4 0.4 copy-done.8
  82.8 133.9 %all-reduce.4.cloned.1.call-done = f32[128,4608]{1,0:T(8,128)} async-done(((f32[128,4608]{1,0:T(8,128)}), f32[128,4608]{1,0:T(8,128)}) %all-reduce.4.cloned.1.call-update) | async-done | bytes 2359312 | tf_op jit(solution)/shard_map/psum | solution.py:86
  216.8 2.1 multiply_reduce_fusion.3
  218.9 0.3 copy-done.2
  219.2 1.9 multiply_reduce_fusion.2
  221.1 2.4 multiply_reduce_fusion
  223.5 9.0 %fusion.4 = f32[128,1152]{1,0:T(8,128)S(1)} fusion(bf16[1152,4608]{1,0:T(8,128)(2,1)} %param.22, f32[128,4608]{1,0:T(8,128)S(1)} %copy-done.2, f32[128,4608]{1,0:T(8,128)} %get-tuple-element.10, f32[128]{0:T(128)S(1)} %broadcast_multiply_fusion.1, f32[128]{0:T(128)S(1)} %get-tuple-element.13, f32[4608]{0:T(1024)S(1)} %copy-done.6, f32[128]{0:T(128)S(1)} %get-tuple-element.14), kind=kOutput, calls=%fused_computation.18 | convolution fusion | flops 1362493440 | bytes 15945216 | tf_op jit(solution)/shard_map/dot_general | solution.py:26
  232.6 3.5 fusion.19
  236.1 9.0 %convolution_add_fusion = f32[128,4608]{1,0:T(8,128)} fusion(f32[128,4608]{1,0:T(8,128)S(1)} %fusion.19, bf16[4608,1152]{1,0:T(8,128)(2,1)} %param.21, f32[128,1152]{1,0:T(8,128)S(1)} %fusion.4, f32[128,1152]{1,0:T(8,128)S(1)} %fusion.17), kind=kOutput, calls=%fused_computation.1 | convolution fusion | flops 1361018880 | bytes 16515072 | tf_op jit(solution)/shard_map/dot_general | solution.py:26
  245.2 0.5 all-gather.9.cloned.1.call-update
  245.7 0.3 all-gather.11.cloned.1.call-start
  246.0 1.7 convert_element_type.30
  247.7 132.1 %all-reduce.6.cloned.1.call-done = f32[128,4608]{1,0:T(8,128)} async-done(((f32[128,4608]{1,0:T(8,128)}), f32[128,4608]{1,0:T(8,128)}) %all-reduce.6.cloned.1.call-update) | async-done | bytes 2359312
  379.9 1.1 multiply_reduce_fusion.5
  381.0 1.8 fusion.26
  382.8 53.1 %all-gather.9.cloned.1.call-done = bf16[32,4,4608]{2,1,0:T(4,128)(2,1)} async-done(((bf16[1,4,4608]{2,1,0:T(4,128)(2,1)}), bf16[32,4,4608]{2,1,0:T(4,128)(2,1)}) %all-gather.9.cloned.1.call-update) | async-done | bytes 1179664 | tf_op jit(solution)/shard_map/all_gather | solution.py:73
  435.9 1.4 reshape.72
  437.4 7.8 %fusion = f32[128,2048]{1,0:T(8,128)S(1)} fusion(bf16[128,4608]{1,0:T(8,128)(2,1)S(1)} %reshape.72, bf16[4608,2048]{1,0:T(8,128)(2,1)} %param.23, f32[2048]{0:T(1024)S(1)} %copy-done.7), kind=kOutput, calls=%fused_computation.4 | convolution fusion | flops 2416443392 | bytes 21110784 | tf_op jit(solution)/shard_map/dot_general | solution.py:112
  445.2 7.9 %fusion.2 = f32[128,2048]{1,0:T(8,128)S(1)} fusion(f32[128,2048]{1,0:T(8,128)S(1)} %fusion, bf16[128,4608]{1,0:T(8,128)(2,1)S(1)} %reshape.70, bf16[4608,2048]{1,0:T(8,128)(2,1)} %param.23, f32[2048]{0:T(1024)S(1)} %copy-done.7), kind=kOutput, calls=%fused_computation.7 | convolution fusion | flops 2416705536 | bytes 22159360 | tf_op jit(solution)/shard_map/dot_general | solution.py:110
  453.0 38.8 %all-gather.11.cloned.1.call-done = bf16[32,4,4608]{2,1,0:T(4,128)(2,1)} async-done(((bf16[1,4,4608]{2,1,0:T(4,128)(2,1)}), bf16[32,4,4608]{2,1,0:T(4,128)(2,1)}) %all-gather.11.cloned.1.call-update) | async-done | bytes 1179664 | tf_op jit(solution)/shard_map/all_gather | solution.py:116
  491.8 1.4 reshape.74
  493.2 13.1 %fusion.3 = f32[2048]{0:T(1024)} fusion(f32[128,2048]{1,0:T(8,128)S(1)} %fusion.2, bf16[128,4608]{1,0:T(8,128)(2,1)S(1)} %reshape.74, bf16[2048,4608]{1,0:T(8,128)(2,1)} %param.25), kind=kOutput, calls=%fused_computation.17 | convolution fusion | flops 2416441344 | bytes 21110784 | tf_op jit(solution)/shard_map/dot_general | solution.py:26
  (48 shorter events, 0.8 us)
Async XLA Ops:
  6.5 212.3 %copy-start = (bf16[128,4608]{1,0:T(8,128)(2,1)S(1)}, bf16[128,4608]{1,0:T(8,128)(2,1)}, u32[]{:S(2)}) copy-start(bf16[128,4608]{1,0:T(8,128)(2,1)} %param.16) | copy-start | bytes 3538948
  6.5 62.4 %copy-start.3 = (f32[4608]{0:T(1024)S(1)}, f32[4608]{0:T(1024)}, u32[]{:S(2)}) copy-start(f32[4608]{0:T(1024)} %param.17) | copy-start | bytes 55300
  6.5 60.6 %all-gather.7.cloned.1.call-start = ((), (), s32[]{:S(2)}) async-start(), calls=%async_computation.1 | async-start | bytes 1216512 | tf_op jit(solution)/shard_map/all_gather | solution.py:72
  7.3 209.5 %all-reduce.4.cloned.1.call-start = ((), (), s32[]{:S(2)}) async-start(), calls=%async_computation | async-start | bytes 4718592 | tf_op jit(solution)/shard_map/psum | solution.py:86
  68.6 6.4 %slice-start.3 = ((s8[10616832]{0:T(1024)(128)(4,1)}), s8[4194304]{0:T(1024)(128)(4,1)S(1)}, s32[]{:S(2)}) async-start(s8[10616832]{0:T(1024)(128)(4,1)} %bitcast.28), calls=%async_computation.8 | async-start | bytes 8388608
  68.9 6.2 %slice-start.4 = ((s8[10616832]{0:T(1024)(128)(4,1)}), s8[4194304]{0:T(1024)(128)(4,1)S(1)}, s32[]{:S(2)}) async-start(s8[10616832]{0:T(1024)(128)(4,1)} %bitcast.28), calls=%async_computation.9 | async-start | bytes 8388608
  68.9 6.9 %slice-start.5 = ((s8[10616832]{0:T(1024)(128)(4,1)}), s8[2228224]{0:T(1024)(128)(4,1)S(1)}, s32[]{:S(2)}) async-start(s8[10616832]{0:T(1024)(128)(4,1)} %bitcast.28), calls=%async_computation.10 | async-start | bytes 4456448
  68.9 6.9 %copy-start.4 = (f32[4608]{0:T(1024)S(1)}, f32[4608]{0:T(1024)}, u32[]{:S(2)}) copy-start(f32[4608]{0:T(1024)} %param.17) | copy-start | bytes 55300
  68.9 8.6 %slice-start.6 = ((s8[10616832]{0:T(1024)(128)(4,1)}), s8[4194304]{0:T(1024)(128)(4,1)S(1)}, s32[]{:S(2)}) async-start(s8[10616832]{0:T(1024)(128)(4,1)} %bitcast.30), calls=%async_computation.11 | async-start | bytes 8388608
  69.0 9.2 %slice-start.7 = ((s8[10616832]{0:T(1024)(128)(4,1)}), s8[4194304]{0:T(1024)(128)(4,1)S(1)}, s32[]{:S(2)}) async-start(s8[10616832]{0:T(1024)(128)(4,1)} %bitcast.30), calls=%async_computation.12 | async-start | bytes 8388608
  75.8 3.2 slice-start.8
  82.2 0.7 copy-start.8
  82.2 297.7 %all-reduce.6.cloned.1.call-start = ((), (), s32[]{:S(2)}) async-start(), calls=%async_computation.4 | async-start | bytes 4718592
  216.8 2.4 copy-start.2
  219.2 1.9 copy-start.6
  221.0 11.5 %slice-start = ((s8[10616832]{0:T(1024)(128)(4,1)}), s8[4194304]{0:T(1024)(128)(4,1)S(1)}, s32[]{:S(2)}) async-start(s8[10616832]{0:T(1024)(128)(4,1)} %bitcast.26), calls=%async_computation.5 | async-start | bytes 8388608
  221.1 11.5 %slice-start.1 = ((s8[10616832]{0:T(1024)(128)(4,1)}), s8[4194304]{0:T(1024)(128)(4,1)S(1)}, s32[]{:S(2)}) async-start(s8[10616832]{0:T(1024)(128)(4,1)} %bitcast.26), calls=%async_computation.6 | async-start | bytes 8388608
  223.5 9.1 %slice-start.2 = ((s8[10616832]{0:T(1024)(128)(4,1)}), s8[2228224]{0:T(1024)(128)(4,1)S(1)}, s32[]{:S(2)}) async-start(s8[10616832]{0:T(1024)(128)(4,1)} %bitcast.26), calls=%async_computation.7 | async-start | bytes 4456448
  245.1 134.8 %copy-start.5 = (f32[4608]{0:T(1024)S(1)}, f32[4608]{0:T(1024)}, u32[]{:S(2)}) copy-start(f32[4608]{0:T(1024)} %param.17) | copy-start | bytes 55300
  245.1 190.8 %all-gather.9.cloned.1.call-start = ((), (), s32[]{:S(2)}) async-start(), calls=%async_computation.2 | async-start | bytes 1216512 | tf_op jit(solution)/shard_map/all_gather | solution.py:73
  245.7 246.1 %all-gather.11.cloned.1.call-start = ((), (), s32[]{:S(2)}) async-start(), calls=%async_computation.3 | async-start | bytes 1216512 | tf_op jit(solution)/shard_map/all_gather | solution.py:116
  246.0 191.4 %copy-start.7 = (f32[2048]{0:T(1024)S(1)}, f32[2048]{0:T(1024)}, u32[]{:S(2)}) copy-start(f32[2048]{0:T(1024)} %param.24) | copy-start | bytes 24580
  493.2 13.1 %copy-start.1 = (bf16[128,4608]{1,0:T(8,128)(2,1)S(1)}, bf16[128,4608]{1,0:T(8,128)(2,1)}, u32[]{:S(2)}) copy-start(bf16[128,4608]{1,0:T(8,128)(2,1)} %param.16) | copy-start | bytes 3538948
Sparse Core Ops, SparseCore 0:
  10.3 56.7 all-gather.6
  82.3 134.4 all-reduce.3
  245.2 134.5 all-reduce.5
  382.7 53.1 all-gather.8
  438.8 52.9 all-gather.10
where the time goes:
time: 513 us
  waiting for transfers between devices  419 us (82%)
  matrix products  63.1 us (12%)
  between operations  13.4 us (3%)
  other arithmetic  9.48 us (2%)
  local copies, waits for them, and re-layouts  7.23 us (1%)
    psum x1, waiting for transfers between devices, local(): lax.psum(jnp.dot(hidden, w_down, preferred_element_type=jnp.float32), ('m...  134 us
    unnamed x6, waiting for transfers between devices  133 us
    all_gather x1, waiting for transfers between devices, local(): lax.all_gather(resid_clean, ('mp', 'latent'), axis=0, tiled=True)  59.9 us
    all_gather x1, waiting for transfers between devices, local(): lax.all_gather(resid_corrupt, ('mp', 'latent'), axis=0, tiled=True)  53.1 us
    all_gather x1, waiting for transfers between devices, local(): lax.all_gather(grad_stream, ('mp', 'latent'), axis=0, tiled=True)  38.8 us
    dot_general x4, matrix products, contract_last(): lax.dot_general(left, right, (((1,), (1,)), ((), ())), preferred_element_...  34.7 us
  transfers between devices with their start and end apart: 5, of which 5 were waited for; matrix products, arithmetic and copies ran while one was open for 4% of the time, Pallas kernels for 0%

commit v1 on v0

--- a/solution.py
+++ b/solution.py
@@ -1,6 +1,10 @@
+import functools
+
 import jax
 import jax.numpy as jnp
 from jax import lax
+from jax.experimental import pallas as pl
+from jax.experimental.pallas import tpu as pltpu
 from jax.sharding import PartitionSpec as P
 
 SEQ = 128
@@ -119,9 +123,348 @@
     return jnp.sum(product.reshape(total_rows // SEQ, SEQ, product.shape[1]), axis=1)
 
 
+MESH = pl.DeviceIdType.MESH
+BF = jnp.bfloat16
+F32 = jnp.float32
+
+
+class Place:
+    def __init__(self, depth):
+        self.depth = depth
+        self.mp = lax.axis_index("mp")
+        self.lat = lax.axis_index("latent")
+        self.c, self.y = self.mp % 2, self.mp // 2
+        self.x, self.z = self.lat % 2, self.lat // 2
+        self.core_peer = (self.y * 2 + 1 - self.c, self.lat)
+        self.mp_y = (1 - self.y) * 2 + self.c
+        self.y_peer = (self.mp_y, self.lat)
+        self.x_peer = (self.mp, self.z * 2 + 1 - self.x)
+
+    def z_peer(self, step):
+        return (self.mp, ((self.z + step) % self.depth) * 2 + self.x)
+
+    def greet(self):
+        barrier = pltpu.get_barrier_semaphore()
+        peers = [self.core_peer, self.y_peer, self.x_peer]
+        peers += [self.z_peer(step) for step in range(1, self.depth)]
+        for peer in peers:
+            pl.semaphore_signal(barrier, inc=1, device_id=peer, device_id_type=MESH)
+        pl.semaphore_wait(barrier, len(peers))
+
+
+class Wires:
+    def __init__(self, send, recv):
+        self.send, self.recv, self.used = send, recv, 0
+
+    def start(self, src, dst, peer):
+        i = self.used
+        self.used += 1
+        copy = pltpu.make_async_remote_copy(
+            src_ref=src, dst_ref=dst, send_sem=self.send.at[i], recv_sem=self.recv.at[i],
+            device_id=peer, device_id_type=MESH,
+        )
+        copy.start()
+        return copy
+
+
+def finish(copies):
+    for copy in copies:
+        copy.wait()
+
+
+def rows16(start):
+    return pl.ds(pl.multiple_of(start, 16), 16)
+
+
+def rows32(start):
+    return pl.ds(pl.multiple_of(start, 32), 32)
+
+
+def gather_blocks(at, wires, own, buf):
+    depth = at.depth
+    cut = (buf.shape[1] // 256) * 128
+    half0, half1 = pl.ds(0, cut), pl.ds(cut, buf.shape[1] - cut)
+    lane = ((at.c * 2 + at.y) * 2 + at.x) * depth
+    quad = depth * 16
+    mine = rows16((lane + at.z) * 16)
+    group = pl.ds(pl.multiple_of(lane * 16, quad), quad)
+    group_y = pl.ds(pl.multiple_of(((at.c * 2 + 1 - at.y) * 2 + at.x) * quad, quad), quad)
+    pair = pl.ds(pl.multiple_of((at.c * 2 + at.y) * 2 * quad, quad), 2 * quad)
+    side = pl.ds(pl.multiple_of(at.c * 4 * quad, quad), 4 * quad)
+    first = [wires.start(own, buf.at[mine], at.z_peer(s)) for s in range(1, depth)]
+    buf[mine, :] = own[...]
+    finish(first)
+    yield
+    cx = wires.start(buf.at[group, half0], buf.at[group, half0], at.x_peer)
+    cy = wires.start(buf.at[group, half1], buf.at[group, half1], at.y_peer)
+    finish([cx, cy])
+    yield
+    cy = wires.start(buf.at[pair, half0], buf.at[pair, half0], at.y_peer)
+    cx = wires.start(buf.at[group, half1], buf.at[group, half1], at.x_peer)
+    cx2 = wires.start(buf.at[group_y, half1], buf.at[group_y, half1], at.x_peer)
+    finish([cy, cx, cx2])
+    yield
+    finish([wires.start(buf.at[side], buf.at[side], at.core_peer)])
+
+
+def gather_rows(at, wires, own, buf):
+    depth = at.depth
+    width = own.shape[1]
+    half = buf.shape[1] // 2
+    halves = (pl.ds(0, half), pl.ds(half, half))
+    mine = rows16((at.mp * 2 + at.x) * 16)
+    other = rows16((at.mp_y * 2 + at.x) * 16)
+    both = rows32(at.mp * 32)
+    both_y = rows32(at.mp_y * 32)
+    spot = buf.at[mine, pl.ds(pl.multiple_of(at.z * width, 128), width)]
+    first = [wires.start(own, spot, at.z_peer(s)) for s in range(1, depth)]
+    buf[mine, pl.ds(pl.multiple_of(at.z * width, 128), width)] = own[...]
+    finish(first)
+    yield
+
+    def share(rows, h, peer):
+        spot = buf.at[rows, halves[h]]
+        return wires.start(spot, spot, peer)
+
+    finish([share(mine, 0, at.x_peer), share(mine, 1, at.y_peer)])
+    yield
+    core = [share(both, 0, at.core_peer)]
+    step = [share(both, 0, at.y_peer), share(mine, 1, at.x_peer), share(other, 1, at.x_peer)]
+    finish(step)
+    yield
+    core += [share(both_y, 0, at.core_peer), share(both, 1, at.core_peer), share(both_y, 1, at.core_peer)]
+    finish(core)
+
+
+def scatter_sum(at, wires, part, bufs, total):
+    rc, s1, ry, s2a, rx, s2b, rx2, ry2, s3, rz = bufs
+    depth = at.depth
+    width = total.shape[1]
+    half = part.shape[1] // 2
+    h0, h1 = pl.ds(0, half), pl.ds(half, half)
+    core = []
+    for h in (h0, h1):
+        for yy in range(2):
+            core.append(wires.start(
+                part.at[rows32((yy * 2 + 1 - at.c) * 32), h], rc.at[yy, :, h], at.core_peer))
+    own16, peer16 = rows16(at.x * 16), rows16((1 - at.x) * 16)
+    yield
+    finish(core[:2])
+    for yy in range(2):
+        s1[yy, :, h0] = (part[rows32((yy * 2 + at.c) * 32), h0].astype(F32) + rc[yy, :, h0].astype(F32)).astype(BF)
+    cy = wires.start(s1.at[1 - at.y, :, h0], ry, at.y_peer)
+    finish(core[2:])
+    for yy in range(2):
+        s1[yy, :, h1] = (part[rows32((yy * 2 + at.c) * 32), h1].astype(F32) + rc[yy, :, h1].astype(F32)).astype(BF)
+    cx = [wires.start(s1.at[yy, peer16, h1], rx.at[yy], at.x_peer) for yy in range(2)]
+    yield
+    finish([cy])
+    s2a[...] = (s1[at.y, :, h0].astype(F32) + ry[...].astype(F32)).astype(BF)
+    cx2 = wires.start(s2a.at[peer16], rx2, at.x_peer)
+    finish(cx)
+    for yy in range(2):
+        s2b[yy] = (s1[yy, own16, h1].astype(F32) + rx[yy].astype(F32)).astype(BF)
+    cy2 = wires.start(s2b.at[1 - at.y], ry2, at.y_peer)
+    yield
+    finish([cx2])
+    s3[:, h0] = (s2a[own16, :].astype(F32) + rx2[...].astype(F32)).astype(BF)
+    finish([cy2])
+    s3[:, h1] = (s2b[at.y].astype(F32) + ry2[...].astype(F32)).astype(BF)
+    last = []
+    for s in range(1, depth):
+        column = pl.multiple_of(((at.z + s) % depth) * width, 128)
+        last.append(wires.start(s3.at[:, pl.ds(column, width)], rz.at[s - 1], at.z_peer(s)))
+    yield
+    finish(last)
+    value = s3[:, pl.ds(pl.multiple_of(at.z * width, 128), width)].astype(F32)
+    for s in range(1, depth):
+        value = value + rz[s - 1].astype(F32)
+    total[...] = value
+
+
+def scatter_buffers(d, depth):
+    half, width = d // 2, d // depth
+    return [
+        pltpu.VMEM((2, 32, d), BF), pltpu.VMEM((2, 32, d), BF), pltpu.VMEM((32, half), BF),
+        pltpu.VMEM((32, half), BF), pltpu.VMEM((2, 16, half), BF), pltpu.VMEM((2, 16, half), BF),
+        pltpu.VMEM((16, half), BF), pltpu.VMEM((16, half), BF), pltpu.VMEM((16, d), BF),
+        pltpu.VMEM((depth - 1, 16, width), BF),
+    ]
+
+
+def share_stats(at, wires, sums, out, inbox):
+    lane = lax.broadcasted_iota(jnp.int32, (16, 128), 1)
+    packed = jnp.zeros((16, 128), F32)
+    for i, value in enumerate(sums):
+        packed = jnp.where(lane == i, value, packed)
+    out[...] = packed
+    finish([wires.start(out, inbox.at[s - 1], at.z_peer(s)) for s in range(1, at.depth)])
+    for s in range(1, at.depth):
+        packed = packed + inbox[s - 1]
+    return [packed[:, i : i + 1] for i in range(len(sums))]
+
+
+def row_sum(value):
+    return jnp.sum(value, axis=-1, keepdims=True)
+
+
+def run(steps):
+    for _ in steps:
+        pass
+
+
+def middle(at, wires, total, stats, inbox, d, clean, answers, unembed, post_gain, final_gain):
+    width = total.shape[1]
+    rows = rows16((at.mp * 2 + at.x) * 16)
+    columns = pl.ds(pl.multiple_of(at.z * width, 128), width)
+    m = total[...]
+    s = clean[rows, columns].astype(F32)
+    pg = post_gain[:, columns]
+    ids = answers[rows, :]
+    candidate = lax.broadcasted_iota(jnp.int32, (16, unembed.shape[0]), 1)
+    selector = (
+        jnp.where(candidate == ids[:, 0:1], 1.0, 0.0) - jnp.where(candidate == ids[:, 1:2], 1.0, 0.0)
+    ).astype(BF)
+    direction = jnp.dot(selector, unembed[:, columns], preferred_element_type=F32)
+    weighted = final_gain[:, columns] * direction
+    mg = m * pg
+    sums = [row_sum(m * m), row_sum(s * s), row_sum(s * mg), row_sum(mg * mg), row_sum(weighted * s), row_sum(weighted * mg)]
+    mm, ss, smg, mgmg, ws, wmg = [v * (1.0 / d) for v in share_stats(at, wires, sums, stats, inbox)]
+    inv_post = lax.rsqrt(mm + epsilon)
+    inv_final = lax.rsqrt(ss + 2.0 * inv_post * smg + inv_post * inv_post * mgmg + epsilon)
+    output = s + mg * inv_post
+    lean = (inv_final * inv_final * inv_final) * (ws + inv_post * wmg)
+    grad_output = inv_final * weighted - output * lean
+    pull = inv_final * wmg - lean * (smg + inv_post * mgmg)
+    grad_mlp = inv_post * (pg * grad_output) - m * (inv_post * inv_post * inv_post) * pull
+    return grad_output, grad_mlp, ss
+
+
+def last_grad(at, wires, total, stats, inbox, d, clean, pre_gain, grad_output, ss):
+    width = total.shape[1]
+    rows = rows16((at.mp * 2 + at.x) * 16)
+    columns = pl.ds(pl.multiple_of(at.z * width, 128), width)
+    s = clean[rows, columns].astype(F32)
+    pre_grad = pre_gain[:, columns] * total[...]
+    inv_pre = lax.rsqrt(ss + epsilon)
+    (ps,) = share_stats(at, wires, [row_sum(pre_grad * s)], stats, inbox)
+    return grad_output + inv_pre * pre_grad - s * (inv_pre * inv_pre * inv_pre) * (ps * (1.0 / d))
+
+
+def first_kernel(depth, own, buf, send, recv):
+    at = Place(depth)
+    at.greet()
+    run(gather_blocks(at, Wires(send, recv), own, buf))
+
+
+def middle_kernel(depth, d, part, clean, answers, unembed, post_gain, final_gain, grads, grad_output_ref, ss_ref, send, recv, total, stats, inbox, own, *bufs):
+    at = Place(depth)
+    at.greet()
+    wires = Wires(send, recv)
+    run(scatter_sum(at, wires, part, bufs, total))
+    grad_output, grad_mlp, ss = middle(at, wires, total, stats, inbox, d, clean, answers, unembed, post_gain, final_gain)
+    grad_output_ref[...] = grad_output
+    own[...] = grad_mlp.astype(BF)
+    ss_ref[...] = jnp.broadcast_to(ss, ss_ref.shape)
+    run(gather_rows(at, wires, own, grads))
+
+
+def last_kernel(depth, d, part, clean, pre_gain, grad_output, ss, grads, send, recv, total, stats, inbox, own, *bufs):
+    at = Place(depth)
+    at.greet()
+    wires = Wires(send, recv)
+    run(scatter_sum(at, wires, part, bufs, total))
+    own[...] = last_grad(at, wires, total, stats, inbox, d, clean, pre_gain, grad_output[...], ss[:, 0:1]).astype(BF)
+    run(gather_rows(at, wires, own, grads))
+
+
+def call(kernel, number, outs, scratch, operands):
+    vmem = pl.BlockSpec(memory_space=pltpu.VMEM)
+    return pl.pallas_call(
+        kernel,
+        out_shape=[jax.ShapeDtypeStruct(*o) for o in outs],
+        in_specs=[vmem] * len(operands),
+        out_specs=[vmem] * len(outs),
+        scratch_shapes=[pltpu.SemaphoreType.DMA((48,)), pltpu.SemaphoreType.DMA((48,))] + scratch,
+        compiler_params=pltpu.CompilerParams(
+            collective_id=number, has_side_effects=True, vmem_limit_bytes=48 * 1024 * 1024
+        ),
+    )(*operands)
+
+
+def staged(
+    depth,
+    resid_clean,
+    resid_corrupt,
+    answer_ids,
+    unembed,
+    pre_gain,
+    post_gain,
+    final_gain,
+    w_gate,
+    w_up,
+    w_down,
+    w_enc,
+    b_enc,
+    w_dec,
+):
+    own_rows, d = resid_clean.shape
+    width = d // depth
+    total_rows = own_rows * depth * 8
+    pieces = 16 // own_rows
+    own = jnp.concatenate([resid_clean.reshape(16, width), resid_corrupt.reshape(16, width)], axis=1)
+    (buf,) = call(functools.partial(first_kernel, depth), 0, [((total_rows * pieces, 2 * width), BF)], [], [own])
+    both = buf.reshape(2, 2, 2, depth, own_rows, pieces, 2, width)
+    both = both.transpose(6, 1, 0, 3, 2, 4, 5, 7).reshape(2 * total_rows, d)
+    clean_all = both[:total_rows]
+    stream = clean_all.astype(F32)
+    inv_pre = lax.rsqrt(jnp.mean(stream * stream, axis=-1, keepdims=True) + epsilon)
+    normed = (stream * inv_pre * pre_gain).astype(BF)
+    gate_pre = jnp.dot(normed, w_gate, preferred_element_type=F32)
+    up_proj = jnp.dot(normed, w_up, preferred_element_type=F32)
+    activated = gelu_tanh(gate_pre)
+    hidden = (activated * up_proj).astype(BF)
+    part = jnp.dot(hidden, w_down, preferred_element_type=F32).astype(BF)
+    scratch = [
+        pltpu.VMEM((16, width), F32), pltpu.VMEM((16, 128), F32), pltpu.VMEM((depth - 1, 16, 128), F32),
+        pltpu.VMEM((16, width), BF),
+    ] + scatter_buffers(d, depth)
+    grad_mlp, grad_output, ss = call(
+        functools.partial(middle_kernel, depth, d), 1,
+        [((total_rows, d), BF), ((16, width), F32), ((16, 128), F32)], scratch,
+        [part, clean_all, answer_ids, unembed, post_gain[None], final_gain[None]],
+    )
+    grad_hidden = contract_last(grad_mlp, w_down)
+    grad_gate = (grad_hidden * up_proj * gelu_slope(gate_pre)).astype(BF)
+    grad_up = (grad_hidden * activated).astype(BF)
+    part = (contract_last(grad_gate, w_gate) + contract_last(grad_up, w_up)).astype(BF)
+    (grad_stream,) = call(
+        functools.partial(last_kernel, depth, d), 2, [((total_rows, d), BF)], scratch,
+        [part, clean_all, pre_gain[None], grad_output, ss],
+    )
+    code = jax.nn.relu(jnp.dot(both, w_enc, preferred_element_type=F32) + b_enc)
+    change = code[:total_rows] - code[total_rows:]
+    product = change * contract_last(grad_stream, w_dec)
+    return jnp.sum(product.reshape(total_rows // SEQ, SEQ, product.shape[1]), axis=1)
+
+
+def fits(mesh, rows, d):
+    depth = mesh.shape["latent"] // 2
+    return (
+        mesh.shape["mp"] == 4 and depth >= 2 and rows == 128 and 16 * mesh.shape["latent"] * 4 == rows * depth
+        and d % (128 * depth) == 0 and d % 256 == 0
+    )
+
+
 def solution(mesh):
+    def chosen(resid_clean, *rest):
+        rows = resid_clean.shape[0] * mesh.shape["mp"] * mesh.shape["latent"]
+        if fits(mesh, rows, resid_clean.shape[1]):
+            return staged(mesh.shape["latent"] // 2, resid_clean, *rest)
+        return local(resid_clean, *rest)
+
     return jax.shard_map(
-        local,
+        chosen,
         mesh=mesh,
         in_specs=(
             P(("mp", "latent"), None),

time: 513 us -> 170 us (0.33)
  waiting for transfers between devices: 419 us -> 0 us
  Pallas kernels: 0 us -> 99 us
  between operations: 13.4 us -> 0.37 us
  other arithmetic: 9.48 us -> 0.88 us
  matrix products: 63.1 us -> 56.8 us
  local copies, waits for them, and re-layouts: 7.23 us -> 12.5 us
    all_gather x3 -> x0, waiting for transfers between devices: 152 us -> none  [the longest x1 59.9 us: local(): lax.all_gather(resid_clean, ('mp', 'latent'), axis=0, tiled=True)]
    psum x1 -> x0, waiting for transfers between devices: 134 us -> none  [local(): lax.psum(jnp.dot(hidden, w_down, preferred_element_type=jnp.float32), ('m...]
    unnamed x6 -> x0, waiting for transfers between devices: 133 us -> none
    pallas_call x0 -> x3, Pallas kernels: none -> 99 us  [call(): pl.pallas_call(kernel, out_shape=[jax.ShapeDtypeStruct(*o) for o in outs]...]
    reshape x0 -> x4, local copies, waits for them, and re-layouts: none -> 6.33 us  [the longest x2 4.73 us: staged(): both = buf.reshape(2, 2, 2, depth, own_rows, pieces, 2, width)]
    dot_general x6 -> x4, matrix products: 28.4 us -> 24.3 us  [the longest x1 10.6 us: staged(): code = jax.nn.relu(jnp.dot(both, w_enc, preferred_element_type=F32) + b_enc)]
  transfers between devices with their start and end apart: 5 -> 0, of which waited for: 5 -> 0; matrix products, arithmetic and copies ran while one was open for 4% -> 0% of each run, Pallas kernels for 0% -> 0%
where the time goes in v1:
time: 170 us
  Pallas kernels  99 us (58%)
  matrix products  56.8 us (33%)
  local copies, waits for them, and re-layouts  12.5 us (7%)
    pallas_call x3, Pallas kernels, call(): pl.pallas_call(kernel, out_shape=[jax.ShapeDtypeStruct(*o) for o in outs]...  99 us
    dot_general x4, matrix products, contract_last(): lax.dot_general(left, right, (((1,), (1,)), ((), ())), preferred_element_...  32.5 us
    dot_general x1, matrix products, staged(): code = jax.nn.relu(jnp.dot(both, w_enc, preferred_element_type=F32) + b_enc)  10.6 us
    dot_general x1, matrix products, staged(): up_proj = jnp.dot(normed, w_up, preferred_element_type=F32)  6 us
    dot_general x1, matrix products, staged(): gate_pre = jnp.dot(normed, w_gate, preferred_element_type=F32)  5.91 us
    reshape x2, local copies, waits for them, and re-layouts, staged(): both = buf.reshape(2, 2, 2, depth, own_rows, pieces, 2, width)  4.73 us
    unnamed x39, local copies, waits for them, and re-layouts  4.11 us

profile of v1, /device:TPU:0, one launch (start us, length us, event | category | flops | bytes accessed | tf_op | source)
XLA Modules:
  0.0 169.6 jit_solution(13918210615669634636)
XLA Ops:
  0.0 0.8 reshape.34
  0.8 0.8 reshape.35
  1.6 26.7 %shard_map.127 = bf16[512,2304]{1,0:T(8,128)(2,1)S(1)} custom-call(bf16[16,2304]{1,0:T(8,128)(2,1)S(1)} %pad_maximum_fusion.own), custom_call_target="tpu_custom_call" | custom-call | tf_op jit(solution)/shard_map/pallas_call | solution.py:383
  28.4 2.2 %reshape.36 = bf16[2,2,2,4,4,4,2,1152]{7,6,5,4,3,2,1,0:T(2,128)(2,1)} reshape(bf16[512,2304]{1,0:T(8,128)(2,1)S(1)} %shard_map.127) | data formatting | bytes 4718592 | tf_op jit(solution)/shard_map/reshape | solution.py:417
  30.5 2.6 %copy.20 = bf16[2,2,2,4,4,4,2,1152]{7,5,4,2,3,0,1,6:T(4,128)(2,1)S(1)} copy(bf16[2,2,2,4,4,4,2,1152]{7,6,5,4,3,2,1,0:T(2,128)(2,1)} %reshape.36) | data formatting | bytes 4718592 | tf_op jit(solution)/shard_map/reshape | solution.py:417
  33.1 0.4 slice.18
  33.6 0.1 copy.17
  33.7 0.8 copy-done.2
  34.5 0.9 multiply_reduce_fusion
  35.4 0.1 rsqrt.12
  35.5 0.0 slice-start.3
  35.5 5.9 %fusion.11 = f32[128,1152]{1,0:T(8,128)S(1)} fusion(bf16[4608,1152]{1,0:T(8,128)(2,1)} %param.20, bf16[128,4608]{1,0:T(8,128)(2,1)S(1)} %bitcast.20, f32[4608]{0:T(1024)S(1)} %copy-done.8, f32[128]{0:T(128)S(1)} %rsqrt.12), kind=kOutput, calls=%fused_computation.23 | convolution fusion | flops 1361313792 | bytes 12405248 | tf_op jit(solution)/shard_map/dot_general | solution.py:423
  41.5 0.0 slice-start.5
  41.5 6.0 %fusion.10 = f32[128,1152]{1,0:T(8,128)S(1)} fusion(bf16[4608,1152]{1,0:T(8,128)(2,1)} %param.21, bf16[128,4608]{1,0:T(8,128)(2,1)S(1)} %bitcast.21, f32[4608]{0:T(1024)S(1)} %copy-done.8, f32[128]{0:T(128)S(1)} %rsqrt.12), kind=kOutput, calls=%fused_computation.22 | convolution fusion | flops 1361313792 | bytes 12405248 | tf_op jit(solution)/shard_map/dot_general | solution.py:424
  47.5 0.8 copy-done.6
  48.3 0.0 copy-start.10
  48.4 1.8 %convolution_convert_fusion.part = bf16[128,4608]{1,0:T(8,128)(2,1)S(1)} fusion(bf16[1152,4608]{1,0:T(8,128)(2,1)S(1)} %bitcast.27, f32[128,1152]{1,0:T(8,128)S(1)} %fusion.10, f32[128,1152]{1,0:T(8,128)S(1)} %fusion.11), kind=kOutput, calls=%fused_computation.1 | convolution fusion | flops 1361018880 | bytes 12976128 | tf_op jit(solution)/shard_map/dot_general | solution.py:427
  50.2 0.7 copy.15.answers
  50.9 0.7 broadcast_in_dim.12.post_gain
  51.6 0.7 broadcast_in_dim.13.final_gain
  52.4 0.8 copy-done.1
  53.2 36.2 %shard_map.128 = (bf16[128,4608]{1,0:T(8,128)(2,1)S(1)}, f32[16,1152]{1,0:T(8,128)S(1)}, f32[16,128]{1,0:T(8,128)S(1)}) custom-call(bf16[128,4608]{1,0:T(8,128)(2,1)S(1)} %convolution_convert_fusion.part, bf16[128,4608]{1,0:T(8,128)(2,1)S(1)} %bitcast.22, s32[128,2]{1,0:T(8,128)S(1)} %copy-done.1, bf16[128,4608]{1,0:T(8,128)(2,1)S(1)} %copy-done, ...), custom_call_target="tpu_custom_call" | custom-call | tf_op jit(solution)/shard_map/pallas_call | solution.py:383
  89.5 0.0 slice-start
  89.5 7.6 %fusion.33 = f32[128,1152]{1,0:T(8,128)S(1)} fusion(bf16[128,4608]{1,0:T(8,128)(2,1)S(1)} %get-tuple-element.8, bf16[1152,4608]{1,0:T(8,128)(2,1)} %param.22), kind=kOutput, calls=%fused_computation.47 | convolution fusion | flops 1358954496 | bytes 12386304 | tf_op jit(solution)/shard_map/dot_general | solution.py:30
  97.1 0.0 slice-start.2
  97.1 7.7 %fusion.12 = f32[128,4608]{1,0:T(8,128)S(1)} fusion(bf16[4608,1152]{1,0:T(8,128)(2,1)} %param.20, f32[128,1152]{1,0:T(8,128)S(1)} %copy-done.5, f32[128,1152]{1,0:T(8,128)S(1)} %fusion.33, f32[128,1152]{1,0:T(8,128)S(1)} %copy-done.7), kind=kOutput, calls=%fused_computation.24 | convolution fusion | flops 1361903616 | bytes 14745600 | tf_op jit(solution)/shard_map/dot_general | solution.py:30
  104.8 3.7 %fusion.part = bf16[128,4608]{1,0:T(8,128)(2,1)S(1)} fusion(f32[128,4608]{1,0:T(8,128)S(1)} %fusion.12, bf16[4608,1152]{1,0:T(8,128)(2,1)S(1)} %bitcast.25, f32[128,1152]{1,0:T(8,128)S(1)} %fusion.33, f32[128,1152]{1,0:T(8,128)S(1)} %copy-done.5), kind=kOutput, calls=%fused_computation.2 | convolution fusion | flops 1361608704 | bytes 15335424 | tf_op jit(solution)/shard_map/dot_general | solution.py:30
  108.6 36.1 %shard_map.129 = bf16[128,4608]{1,0:T(8,128)(2,1)S(1)} custom-call(bf16[128,4608]{1,0:T(8,128)(2,1)S(1)} %fusion.part, bf16[128,4608]{1,0:T(8,128)(2,1)S(1)} %bitcast.23, f32[1,4608]{1,0:T(1,128)S(1)} %broadcast_in_dim.14.pre_gain, f32[16,1152]{1,0:T(8,128)S(1)} %get-tuple-element.9.grad_output, f32[16,128]{1,0:T(8,128)S(1)} %get-tuple-element.10.ss), custom_call_target="tpu_custom_call" | custom-call | tf_op jit(solution)/shard_map/pallas_call | solution.py:383
  144.7 0.3 copy.16
  145.0 0.4 copy-done.11
  145.3 10.6 %fusion.1 = f32[256,2048]{1,0:T(8,128)} fusion(bf16[256,4608]{1,0:T(8,128)(2,1)S(1)} %bitcast.32, bf16[4608,2048]{1,0:T(8,128)(2,1)} %param.23, f32[2048]{0:T(1024)S(1)} %copy-done.11), kind=kOutput, calls=%fused_computation.4 | convolution fusion | flops 4832886784 | bytes 23339008 | tf_op jit(solution)/shard_map/dot_general | solution.py:445
  156.0 13.6 %fusion.2 = f32[2048]{0:T(1024)} fusion(bf16[128,4608]{1,0:T(8,128)(2,1)S(1)} %shard_map.129, bf16[2048,4608]{1,0:T(8,128)(2,1)} %param.25, f32[256,2048]{1,0:T(8,128)} %fusion.1), kind=kOutput, calls=%fused_computation.8 | convolution fusion | flops 2416703488 | bytes 22159360 | tf_op jit(solution)/shard_map/dot_general | solution.py:30
  (32 shorter events, 0.1 us)
Async XLA Ops:
  33.1 1.4 copy-start.2
  33.5 2.0 %copy-start.8 = (f32[4608]{0:T(1024)S(1)}, f32[4608]{0:T(1024)}, u32[]{:S(2)}) copy-start(f32[4608]{0:T(1024)} %param.17) | copy-start | bytes 55300
  35.5 12.8 %slice-start.3 = ((s8[10616832]{0:T(1024)(128)(4,1)}), s8[4194304]{0:T(1024)(128)(4,1)S(1)}, s32[]{:S(2)}) async-start(s8[10616832]{0:T(1024)(128)(4,1)} %bitcast.26), calls=%async_computation.3 | async-start | bytes 8388608
  35.5 12.8 %slice-start.4 = ((s8[10616832]{0:T(1024)(128)(4,1)}), s8[4194304]{0:T(1024)(128)(4,1)S(1)}, s32[]{:S(2)}) async-start(s8[10616832]{0:T(1024)(128)(4,1)} %bitcast.26), calls=%async_computation.4 | async-start | bytes 8388608
  41.5 6.0 %copy-start.4 = (f32[128,1152]{1,0:T(8,128)}, f32[128,1152]{1,0:T(8,128)S(1)}, u32[]{:S(2)}) copy-start(f32[128,1152]{1,0:T(8,128)S(1)} %fusion.11) | copy-start | bytes 1769476
  41.5 6.9 %slice-start.5 = ((s8[10616832]{0:T(1024)(128)(4,1)}), s8[2228224]{0:T(1024)(128)(4,1)S(1)}, s32[]{:S(2)}) async-start(s8[10616832]{0:T(1024)(128)(4,1)} %bitcast.26), calls=%async_computation.5 | async-start | bytes 4456448
  47.5 0.8 copy-start.6
  48.3 1.8 %copy-start.10 = (s32[128,2]{0,1:T(2,128)S(1)}, s32[128,2]{0,1:T(2,128)}, u32[]{:S(2)}) copy-start(s32[128,2]{0,1:T(2,128)} %param.15) | copy-start | bytes 3076
  48.4 4.0 %copy-start = (bf16[128,4608]{1,0:T(8,128)(2,1)S(1)}, bf16[128,4608]{1,0:T(8,128)(2,1)}, u32[]{:S(2)}) copy-start(bf16[128,4608]{1,0:T(8,128)(2,1)} %unembed.1) | copy-start | bytes 3538948
  52.4 0.8 copy-start.1
  89.5 7.6 %copy-start.5 = (f32[128,1152]{1,0:T(8,128)S(1)}, f32[128,1152]{1,0:T(8,128)}, u32[]{:S(2)}) copy-start(f32[128,1152]{1,0:T(8,128)} %copy-done.4) | copy-start | bytes 1769476
  89.5 7.6 %copy-start.7 = (f32[128,1152]{1,0:T(8,128)S(1)}, f32[128,1152]{1,0:T(8,128)}, u32[]{:S(2)}) copy-start(f32[128,1152]{1,0:T(8,128)} %copy-done.6) | copy-start | bytes 1769476
  89.5 15.3 %slice-start = ((s8[10616832]{0:T(1024)(128)(4,1)}), s8[4194304]{0:T(1024)(128)(4,1)S(1)}, s32[]{:S(2)}) async-start(s8[10616832]{0:T(1024)(128)(4,1)} %bitcast.24), calls=%async_computation | async-start | bytes 8388608
  89.5 15.3 %slice-start.1 = ((s8[10616832]{0:T(1024)(128)(4,1)}), s8[4194304]{0:T(1024)(128)(4,1)S(1)}, s32[]{:S(2)}) async-start(s8[10616832]{0:T(1024)(128)(4,1)} %bitcast.24), calls=%async_computation.1 | async-start | bytes 8388608
  97.1 7.7 %slice-start.2 = ((s8[10616832]{0:T(1024)(128)(4,1)}), s8[2228224]{0:T(1024)(128)(4,1)S(1)}, s32[]{:S(2)}) async-start(s8[10616832]{0:T(1024)(128)(4,1)} %bitcast.24), calls=%async_computation.2 | async-start | bytes 4456448
  104.8 3.7 %copy-start.9 = (f32[4608]{0:T(1024)S(1)}, f32[4608]{0:T(1024)}, u32[]{:S(2)}) copy-start(f32[4608]{0:T(1024)} %param.17) | copy-start | bytes 55300
  108.5 36.1 %copy-start.3 = (bf16[2,2,2,4,4,4,2,1152]{7,5,4,2,3,0,1,6:T(4,128)(2,1)S(1)}, bf16[2,2,2,4,4,4,2,1152]{7,5,4,2,3,0,1,6:T(4,128)(2,1)}, u32[]{:S(2)}) copy-start(bf16[2,2,2,4,4,4,2,1152]{7,5,4,2,3,0,1,6:T(4,128)(2,1)} %copy-done.2) | copy-start | bytes 7077892
  144.6 0.7 copy-start.11

commit v2 on v1

--- a/solution.py
+++ b/solution.py
@@ -193,18 +193,20 @@
     side = pl.ds(pl.multiple_of(at.c * 4 * quad, quad), 4 * quad)
     first = [wires.start(own, buf.at[mine], at.z_peer(s)) for s in range(1, depth)]
     buf[mine, :] = own[...]
+    yield
     finish(first)
-    yield
     cx = wires.start(buf.at[group, half0], buf.at[group, half0], at.x_peer)
     cy = wires.start(buf.at[group, half1], buf.at[group, half1], at.y_peer)
+    yield
     finish([cx, cy])
-    yield
     cy = wires.start(buf.at[pair, half0], buf.at[pair, half0], at.y_peer)
     cx = wires.start(buf.at[group, half1], buf.at[group, half1], at.x_peer)
     cx2 = wires.start(buf.at[group_y, half1], buf.at[group_y, half1], at.x_peer)
+    yield
     finish([cy, cx, cx2])
-    yield
-    finish([wires.start(buf.at[side], buf.at[side], at.core_peer)])
+    core = wires.start(buf.at[side], buf.at[side], at.core_peer)
+    yield
+    finish([core])
 
 
 def gather_rows(at, wires, own, buf):
@@ -219,31 +221,34 @@
     spot = buf.at[mine, pl.ds(pl.multiple_of(at.z * width, 128), width)]
     first = [wires.start(own, spot, at.z_peer(s)) for s in range(1, depth)]
     buf[mine, pl.ds(pl.multiple_of(at.z * width, 128), width)] = own[...]
+    yield
     finish(first)
-    yield
 
     def share(rows, h, peer):
         spot = buf.at[rows, halves[h]]
         return wires.start(spot, spot, peer)
 
-    finish([share(mine, 0, at.x_peer), share(mine, 1, at.y_peer)])
-    yield
+    step = [share(mine, 0, at.x_peer), share(mine, 1, at.y_peer)]
+    yield
+    finish(step)
     core = [share(both, 0, at.core_peer)]
     step = [share(both, 0, at.y_peer), share(mine, 1, at.x_peer), share(other, 1, at.x_peer)]
+    yield
     finish(step)
-    yield
     core += [share(both_y, 0, at.core_peer), share(both, 1, at.core_peer), share(both_y, 1, at.core_peer)]
+    yield
     finish(core)
 
 
-def scatter_sum(at, wires, part, bufs, total):
+def scatter_sum(at, wires, part, bufs, total, produce):
     rc, s1, ry, s2a, rx, s2b, rx2, ry2, s3, rz = bufs
     depth = at.depth
     width = total.shape[1]
     half = part.shape[1] // 2
     h0, h1 = pl.ds(0, half), pl.ds(half, half)
     core = []
-    for h in (h0, h1):
+    for i, h in enumerate((h0, h1)):
+        produce(i)
         for yy in range(2):
             core.append(wires.start(
                 part.at[rows32((yy * 2 + 1 - at.c) * 32), h], rc.at[yy, :, h], at.core_peer))
@@ -308,9 +313,10 @@
     return jnp.sum(value, axis=-1, keepdims=True)
 
 
-def run(steps):
+def run(steps, work=()):
+    work = iter(work)
     for _ in steps:
-        pass
+        next(work, None)
 
 
 def middle(at, wires, total, stats, inbox, d, clean, answers, unembed, post_gain, final_gain):
@@ -351,45 +357,131 @@
     return grad_output + inv_pre * pre_grad - s * (inv_pre * inv_pre * inv_pre) * (ps * (1.0 / d))
 
 
-def first_kernel(depth, own, buf, send, recv):
-    at = Place(depth)
-    at.greet()
-    run(gather_blocks(at, Wires(send, recv), own, buf))
-
-
-def middle_kernel(depth, d, part, clean, answers, unembed, post_gain, final_gain, grads, grad_output_ref, ss_ref, send, recv, total, stats, inbox, own, *bufs):
+def whole_kernel(
+    depth, pieces, own_clean, own_corrupt, target, answers, gains, b_enc, unembed_hbm, wg_hbm, wu_hbm, wd_hbm, we_hbm, wl_hbm, out,
+    send, recv, load, wg, wu, wd, we, wl, unembed, buf0, buf1, xs, normed, gate_pre, up, hidden, grad_gate, grad_up,
+    part, grads, change, kept, total, stats, inbox, own, *bufs,
+):
+    d, units = wg.shape
+    latents = out.shape[1]
+    rows = normed.shape[0]
+    width = d // depth
+    tile = we.shape[2]
+    first = latents // 2
+    pre_gain, post_gain, final_gain = gains.at[0:1], gains.at[1:2], gains.at[2:3]
+    loads = [
+        pltpu.make_async_copy(wg_hbm, wg, load.at[0]),
+        pltpu.make_async_copy(wu_hbm, wu, load.at[1]),
+        pltpu.make_async_copy(wd_hbm, wd, load.at[2]),
+        pltpu.make_async_copy(unembed_hbm, unembed, load.at[3]),
+        pltpu.make_async_copy(wl_hbm.at[first:latents], wl, load.at[4]),
+    ]
+    low = pltpu.make_async_copy(wl_hbm.at[0:first], wd.at[0:first], load.at[5])
+    count = latents // tile
+
+    def piece(p):
+        return pltpu.make_async_copy(we_hbm.at[:, p * tile : (p + 1) * tile], we.at[p % 2], load.at[6 + p % 2])
+
+    for copy in loads[:4]:
+        copy.start()
     at = Place(depth)
     at.greet()
     wires = Wires(send, recv)
-    run(scatter_sum(at, wires, part, bufs, total))
-    grad_output, grad_mlp, ss = middle(at, wires, total, stats, inbox, d, clean, answers, unembed, post_gain, final_gain)
-    grad_output_ref[...] = grad_output
+    run(gather_blocks(at, wires, own_clean, buf0))
+    piece(0).start()
+    piece(1).start()
+    loads[4].start()
+    side = gather_blocks(at, wires, own_corrupt, buf1)
+    next(side, None)
+
+    def arrange(buf, base):
+        place = lax.broadcasted_iota(jnp.int32, (rows, rows * pieces), 1)
+        for s in range(depth):
+            pick = jnp.where(place == target[...] + s, 1.0, 0.0).astype(BF)
+            xs[base : base + rows, s * width : (s + 1) * width] = jnp.dot(pick, buf[...], preferred_element_type=F32).astype(BF)
+
+    arrange(buf0, 0)
+
+    @pl.loop(0, rows // 16)
+    def _(i):
+        span = rows16(i * 16)
+        stream = xs[span, :].astype(F32)
+        inv_pre = lax.rsqrt(row_sum(stream * stream) * (1.0 / d) + epsilon)
+        normed[span, :] = (stream * inv_pre * pre_gain[...]).astype(BF)
+
+    next(side, None)
+    loads[0].wait()
+    loads[1].wait()
+    cuts = [(a, min(a + 256, units)) for a in range(0, units, 256)]
+    for n, (a, b) in enumerate(cuts):
+        gate = jnp.dot(normed[...], wg[:, a:b], preferred_element_type=F32)
+        lift = jnp.dot(normed[...], wu[:, a:b], preferred_element_type=F32)
+        gate_pre[:, a:b] = gate
+        up[:, a:b] = lift
+        hidden[:, a:b] = (gelu_tanh(gate) * lift).astype(BF)
+        if n % 2 == 1:
+            next(side, None)
+    for _ in side:
+        pass
+    loads[2].wait()
+    half = d // 2
+
+    def forward(h):
+        @pl.loop(0, half // 256)
+        def _(i):
+            span = pl.ds(pl.multiple_of(h * half + i * 256, 256), 256)
+            part[:, span] = jnp.dot(hidden[...], wd[:, span], preferred_element_type=F32).astype(BF)
+
+    def encode():
+        for p in range(count):
+            if p == 0:
+                arrange(buf1, rows)
+            piece(p).wait()
+            span = slice(p * tile, (p + 1) * tile)
+            code = jnp.dot(xs[...], we[p % 2], preferred_element_type=F32) + b_enc[:, span]
+            code = jnp.maximum(code, 0.0)
+            change[:, span] = code[:rows] - code[rows:]
+            if p + 2 < count:
+                piece(p + 2).start()
+            yield
+
+    clean = xs.at[0:rows]
+    work = encode()
+    run(scatter_sum(at, wires, part, bufs, total, forward), work)
+    loads[3].wait()
+    grad_output, grad_mlp, ss = middle(
+        at, wires, total, stats, inbox, d, clean, answers, unembed, post_gain, final_gain
+    )
+    kept[...] = grad_output
     own[...] = grad_mlp.astype(BF)
-    ss_ref[...] = jnp.broadcast_to(ss, ss_ref.shape)
-    run(gather_rows(at, wires, own, grads))
-
-
-def last_kernel(depth, d, part, clean, pre_gain, grad_output, ss, grads, send, recv, total, stats, inbox, own, *bufs):
-    at = Place(depth)
-    at.greet()
-    wires = Wires(send, recv)
-    run(scatter_sum(at, wires, part, bufs, total))
-    own[...] = last_grad(at, wires, total, stats, inbox, d, clean, pre_gain, grad_output[...], ss[:, 0:1]).astype(BF)
-    run(gather_rows(at, wires, own, grads))
-
-
-def call(kernel, number, outs, scratch, operands):
-    vmem = pl.BlockSpec(memory_space=pltpu.VMEM)
-    return pl.pallas_call(
-        kernel,
-        out_shape=[jax.ShapeDtypeStruct(*o) for o in outs],
-        in_specs=[vmem] * len(operands),
-        out_specs=[vmem] * len(outs),
-        scratch_shapes=[pltpu.SemaphoreType.DMA((48,)), pltpu.SemaphoreType.DMA((48,))] + scratch,
-        compiler_params=pltpu.CompilerParams(
-            collective_id=number, has_side_effects=True, vmem_limit_bytes=48 * 1024 * 1024
-        ),
-    )(*operands)
+    run(gather_rows(at, wires, own, grads), work)
+    for a, b in cuts:
+        grad_hidden = contract_last(grads[...], wd[a:b, :])
+        gate = gate_pre[:, a:b]
+        grad_gate[:, a:b] = (grad_hidden * up[:, a:b] * gelu_slope(gate)).astype(BF)
+        grad_up[:, a:b] = (grad_hidden * gelu_tanh(gate)).astype(BF)
+    low.start()
+
+    def backward(h):
+        @pl.loop(0, half // 256)
+        def _(i):
+            span = pl.ds(pl.multiple_of(h * half + i * 256, 256), 256)
+            value = contract_last(grad_gate[...], wg[span, :]) + contract_last(grad_up[...], wu[span, :])
+            part[:, span] = value.astype(BF)
+
+    run(scatter_sum(at, wires, part, bufs, total, backward), work)
+    own[...] = last_grad(at, wires, total, stats, inbox, d, clean, pre_gain, kept[...], ss).astype(BF)
+    run(gather_rows(at, wires, own, grads), work)
+    for _ in work:
+        pass
+    low.wait()
+    loads[4].wait()
+    for p in range(count):
+        source = wd if (p + 1) * tile <= first else wl
+        base = p * tile % first
+        projected = contract_last(grads[...], source[base : base + tile, :])
+        span = slice(p * tile, (p + 1) * tile)
+        out[:, span] = jnp.sum(change[:, span] * projected, axis=0, keepdims=True)
 
 
 def staged(
@@ -410,56 +502,58 @@
 ):
     own_rows, d = resid_clean.shape
     width = d // depth
-    total_rows = own_rows * depth * 8
+    units = w_gate.shape[1]
+    latents = w_enc.shape[1]
+    rows = own_rows * depth * 8
     pieces = 16 // own_rows
-    own = jnp.concatenate([resid_clean.reshape(16, width), resid_corrupt.reshape(16, width)], axis=1)
-    (buf,) = call(functools.partial(first_kernel, depth), 0, [((total_rows * pieces, 2 * width), BF)], [], [own])
-    both = buf.reshape(2, 2, 2, depth, own_rows, pieces, 2, width)
-    both = both.transpose(6, 1, 0, 3, 2, 4, 5, 7).reshape(2 * total_rows, d)
-    clean_all = both[:total_rows]
-    stream = clean_all.astype(F32)
-    inv_pre = lax.rsqrt(jnp.mean(stream * stream, axis=-1, keepdims=True) + epsilon)
-    normed = (stream * inv_pre * pre_gain).astype(BF)
-    gate_pre = jnp.dot(normed, w_gate, preferred_element_type=F32)
-    up_proj = jnp.dot(normed, w_up, preferred_element_type=F32)
-    activated = gelu_tanh(gate_pre)
-    hidden = (activated * up_proj).astype(BF)
-    part = jnp.dot(hidden, w_down, preferred_element_type=F32).astype(BF)
+    tile = 256
+    token = jnp.arange(rows, dtype=jnp.int32)[:, None]
+    device = token // own_rows
+    x, z = device % 2, device // 2 % depth
+    c, y = device // (2 * depth) % 2, device // (4 * depth)
+    target = (((c * 2 + y) * 2 + x) * depth + z) * 16 + token % own_rows * pieces
+    vmem = pl.BlockSpec(memory_space=pltpu.VMEM)
+    hbm = pl.BlockSpec(memory_space=pl.ANY)
     scratch = [
-        pltpu.VMEM((16, width), F32), pltpu.VMEM((16, 128), F32), pltpu.VMEM((depth - 1, 16, 128), F32),
-        pltpu.VMEM((16, width), BF),
+        pltpu.SemaphoreType.DMA((80,)), pltpu.SemaphoreType.DMA((80,)), pltpu.SemaphoreType.DMA((8,)),
+        pltpu.VMEM((d, units), BF), pltpu.VMEM((d, units), BF), pltpu.VMEM((units, d), BF),
+        pltpu.VMEM((2, d, tile), BF), pltpu.VMEM((latents // 2, d), BF), pltpu.VMEM(unembed.shape, BF),
+        pltpu.VMEM((rows * pieces, width), BF), pltpu.VMEM((rows * pieces, width), BF),
+        pltpu.VMEM((2 * rows, d), BF), pltpu.VMEM((rows, d), BF),
+        pltpu.VMEM((rows, units), F32), pltpu.VMEM((rows, units), F32), pltpu.VMEM((rows, units), BF),
+        pltpu.VMEM((rows, units), BF), pltpu.VMEM((rows, units), BF),
+        pltpu.VMEM((rows, d), BF), pltpu.VMEM((rows, d), BF), pltpu.VMEM((rows, latents), F32),
+        pltpu.VMEM((16, width), F32), pltpu.VMEM((16, width), F32), pltpu.VMEM((16, 128), F32),
+        pltpu.VMEM((depth - 1, 16, 128), F32), pltpu.VMEM((16, width), BF),
     ] + scatter_buffers(d, depth)
-    grad_mlp, grad_output, ss = call(
-        functools.partial(middle_kernel, depth, d), 1,
-        [((total_rows, d), BF), ((16, width), F32), ((16, 128), F32)], scratch,
-        [part, clean_all, answer_ids, unembed, post_gain[None], final_gain[None]],
-    )
-    grad_hidden = contract_last(grad_mlp, w_down)
-    grad_gate = (grad_hidden * up_proj * gelu_slope(gate_pre)).astype(BF)
-    grad_up = (grad_hidden * activated).astype(BF)
-    part = (contract_last(grad_gate, w_gate) + contract_last(grad_up, w_up)).astype(BF)
-    (grad_stream,) = call(
-        functools.partial(last_kernel, depth, d), 2, [((total_rows, d), BF)], scratch,
-        [part, clean_all, pre_gain[None], grad_output, ss],
-    )
-    code = jax.nn.relu(jnp.dot(both, w_enc, preferred_element_type=F32) + b_enc)
-    change = code[:total_rows] - code[total_rows:]
-    product = change * contract_last(grad_stream, w_dec)
-    return jnp.sum(product.reshape(total_rows // SEQ, SEQ, product.shape[1]), axis=1)
-
-
-def fits(mesh, rows, d):
+    return pl.pallas_call(
+        functools.partial(whole_kernel, depth, pieces),
+        out_shape=jax.ShapeDtypeStruct((1, latents), F32),
+        in_specs=[vmem] * 6 + [hbm] * 6,
+        out_specs=vmem,
+        scratch_shapes=scratch,
+        compiler_params=pltpu.CompilerParams(
+            collective_id=0, has_side_effects=True, vmem_limit_bytes=67043328
+        ),
+    )(
+        resid_clean.reshape(16, width), resid_corrupt.reshape(16, width), target, answer_ids,
+        jnp.stack([pre_gain, post_gain, final_gain]), b_enc[None], unembed, w_gate, w_up, w_down, w_enc, w_dec,
+    )
+
+
+def fits(mesh, rows, d, units, latents):
     depth = mesh.shape["latent"] // 2
     return (
         mesh.shape["mp"] == 4 and depth >= 2 and rows == 128 and 16 * mesh.shape["latent"] * 4 == rows * depth
-        and d % (128 * depth) == 0 and d % 256 == 0
+        and d % (128 * depth) == 0 and d % 512 == 0
+        and rows == SEQ and units % 128 == 0 and latents % 512 == 0 and latents // 2 <= units
     )
 
 
 def solution(mesh):
     def chosen(resid_clean, *rest):
         rows = resid_clean.shape[0] * mesh.shape["mp"] * mesh.shape["latent"]
-        if fits(mesh, rows, resid_clean.shape[1]):
+        if fits(mesh, rows, resid_clean.shape[1], rest[6].shape[1], rest[9].shape[1]):
             return staged(mesh.shape["latent"] // 2, resid_clean, *rest)
         return local(resid_clean, *rest)
 

time: 170 us -> 138 us (0.81)
  matrix products: 56.8 us -> 0 us
  Pallas kernels: 99 us -> 128 us
  local copies, waits for them, and re-layouts: 12.5 us -> 7.75 us
    dot_general x8 -> x0, matrix products: 56.8 us -> none  [the longest x4 32.5 us: contract_last(): lax.dot_general(left, right, (((1,), (1,)), ((), ())), preferred_element_...]
    pallas_call x3 -> x1, Pallas kernels: 99 us -> 128 us  [staged(): pl.pallas_call(functools.partial(whole_kernel, depth, pieces), out_shape=...]
    reshape x2 -> x0, local copies, waits for them, and re-layouts: 4.73 us -> none  [staged(): both = buf.reshape(2, 2, 2, depth, own_rows, pieces, 2, width)]
    another operation x0 -> x3, local copies, waits for them, and re-layouts: none -> 2.23 us  [staged(): jnp.stack([pre_gain, post_gain, final_gain])]
    unnamed x39 -> x2, local copies, waits for them, and re-layouts: 4.11 us -> 2.71 us
where the time goes in v2:
time: 138 us; the launch traced here: 137 us
  Pallas kernels  128 us (93%)
  local copies, waits for them, and re-layouts  7.75 us (6%)
    pallas_call x1, Pallas kernels, staged(): pl.pallas_call(functools.partial(whole_kernel, depth, pieces), out_shape=...  128 us

profile of v2, /device:TPU:0, one launch (start us, length us, event | category | flops | bytes accessed | tf_op | source)
XLA Modules:
  0.0 137.1 jit_solution(9034872490262196177)
XLA Ops:
  0.0 0.7 stack.12
  0.7 0.7 stack.13
  1.5 0.7 stack.14
  2.2 0.7 pad_maximum_fusion.gains
  2.9 1.4 %reshape.382.own_clean = bf16[16,1152]{1,0:T(8,128)(2,1)} reshape(bf16[4,4608]{1,0:T(4,128)(2,1)} %param.13) | data formatting | bytes 73728 | tf_op jit(solution)/shard_map/reshape | solution.py:539
  4.3 1.4 %reshape.383.own_corrupt = bf16[16,1152]{1,0:T(8,128)(2,1)} reshape(bf16[4,4608]{1,0:T(4,128)(2,1)} %param.14) | data formatting | bytes 73728 | tf_op jit(solution)/shard_map/reshape | solution.py:539
  5.7 1.4 %copy.14.answers = s32[128,2]{1,0:T(8,128)} copy(s32[128,2]{0,1:T(2,128)} %param.15) | data formatting | bytes 2048 | tf_op args[2]
  7.1 0.7 fusion.15.target
  7.8 127.9 %shard_map.127 = f32[1,2048]{1,0:T(1,128)} custom-call(bf16[16,1152]{1,0:T(8,128)(2,1)} %reshape.382.own_clean, bf16[16,1152]{1,0:T(8,128)(2,1)} %reshape.383.own_corrupt, s32[128,1]{1,0:T(8,128)} %fusion.15.target, s32[128,2]{1,0:T(8,128)} %copy.14.answers, f32[3,4608]{1,0:T(4,128)} %pad_maximum_fusion.gains, f32[1,2048]{1,0:T(1,128)} %bitcast.1, ...), custom_call_target="tpu_custom_call" | custom-call | tf_op jit(solution)/shard_map/pallas_call | solution.py:529
  135.8 1.3 copy.16

commit v3 on v2

--- a/solution.py
+++ b/solution.py
@@ -2,6 +2,7 @@
 
 import jax
 import jax.numpy as jnp
+import numpy as np
 from jax import lax
 from jax.experimental import pallas as pl
 from jax.experimental.pallas import tpu as pltpu
@@ -229,13 +230,16 @@
         return wires.start(spot, spot, peer)
 
     step = [share(mine, 0, at.x_peer), share(mine, 1, at.y_peer)]
+    core = [share(mine, 0, at.core_peer), share(mine, 1, at.core_peer)]
     yield
     finish(step)
-    core = [share(both, 0, at.core_peer)]
+    near = rows16((at.mp * 2 + 1 - at.x) * 16)
+    far = rows16((at.mp_y * 2 + 1 - at.x) * 16)
     step = [share(both, 0, at.y_peer), share(mine, 1, at.x_peer), share(other, 1, at.x_peer)]
+    core += [share(near, 0, at.core_peer), share(other, 1, at.core_peer)]
     yield
     finish(step)
-    core += [share(both_y, 0, at.core_peer), share(both, 1, at.core_peer), share(both_y, 1, at.core_peer)]
+    core += [share(both_y, 0, at.core_peer), share(near, 1, at.core_peer), share(far, 1, at.core_peer)]
     yield
     finish(core)
 
@@ -246,21 +250,29 @@
     width = total.shape[1]
     half = part.shape[1] // 2
     h0, h1 = pl.ds(0, half), pl.ds(half, half)
-    core = []
-    for i, h in enumerate((h0, h1)):
-        produce(i)
+    own16, peer16 = rows16(at.x * 16), rows16((1 - at.x) * 16)
+
+    def swap(h):
+        return [
+            wires.start(part.at[rows32((yy * 2 + 1 - at.c) * 32), h], rc.at[yy, :, h], at.core_peer)
+            for yy in range(2)
+        ]
+
+    def merge(h):
         for yy in range(2):
-            core.append(wires.start(
-                part.at[rows32((yy * 2 + 1 - at.c) * 32), h], rc.at[yy, :, h], at.core_peer))
-    own16, peer16 = rows16(at.x * 16), rows16((1 - at.x) * 16)
-    yield
-    finish(core[:2])
-    for yy in range(2):
-        s1[yy, :, h0] = (part[rows32((yy * 2 + at.c) * 32), h0].astype(F32) + rc[yy, :, h0].astype(F32)).astype(BF)
+            s1[yy, :, h] = (part[rows32((yy * 2 + at.c) * 32), h].astype(F32) + rc[yy, :, h].astype(F32)).astype(BF)
+
+    produce(0, 2)
+    core0 = swap(h0)
+    produce(2, 3)
+    finish(core0)
+    merge(h0)
     cy = wires.start(s1.at[1 - at.y, :, h0], ry, at.y_peer)
-    finish(core[2:])
-    for yy in range(2):
-        s1[yy, :, h1] = (part[rows32((yy * 2 + at.c) * 32), h1].astype(F32) + rc[yy, :, h1].astype(F32)).astype(BF)
+    produce(3, 4)
+    core1 = swap(h1)
+    yield
+    finish(core1)
+    merge(h1)
     cx = [wires.start(s1.at[yy, peer16, h1], rx.at[yy], at.x_peer) for yy in range(2)]
     yield
     finish([cy])
@@ -424,12 +436,10 @@
     for _ in side:
         pass
     loads[2].wait()
-    half = d // 2
-
-    def forward(h):
-        @pl.loop(0, half // 256)
+    def forward(low_quarter, high_quarter):
+        @pl.loop(d // 256 * low_quarter // 4, d // 256 * high_quarter // 4)
         def _(i):
-            span = pl.ds(pl.multiple_of(h * half + i * 256, 256), 256)
+            span = pl.ds(pl.multiple_of(i * 256, 256), 256)
             part[:, span] = jnp.dot(hidden[...], wd[:, span], preferred_element_type=F32).astype(BF)
 
     def encode():
@@ -462,10 +472,10 @@
         grad_up[:, a:b] = (grad_hidden * gelu_tanh(gate)).astype(BF)
     low.start()
 
-    def backward(h):
-        @pl.loop(0, half // 256)
+    def backward(low_quarter, high_quarter):
+        @pl.loop(d // 256 * low_quarter // 4, d // 256 * high_quarter // 4)
         def _(i):
-            span = pl.ds(pl.multiple_of(h * half + i * 256, 256), 256)
+            span = pl.ds(pl.multiple_of(i * 256, 256), 256)
             value = contract_last(grad_gate[...], wg[span, :]) + contract_last(grad_up[...], wu[span, :])
             part[:, span] = value.astype(BF)
 
@@ -507,11 +517,12 @@
     rows = own_rows * depth * 8
     pieces = 16 // own_rows
     tile = 256
-    token = jnp.arange(rows, dtype=jnp.int32)[:, None]
+    token = np.arange(rows, dtype=np.int32)[:, None]
     device = token // own_rows
     x, z = device % 2, device // 2 % depth
     c, y = device // (2 * depth) % 2, device // (4 * depth)
     target = (((c * 2 + y) * 2 + x) * depth + z) * 16 + token % own_rows * pieces
+    target = jnp.asarray(target.astype(np.int32))
     vmem = pl.BlockSpec(memory_space=pltpu.VMEM)
     hbm = pl.BlockSpec(memory_space=pl.ANY)
     scratch = [

time: 138 us -> 138 us (level)
  no operation moved by 1% of the time
where the time goes in v3:
time: 138 us; the launch traced here: 137 us
  Pallas kernels  129 us (93%)
  local copies, waits for them, and re-layouts  7.72 us (6%)
    pallas_call x1, Pallas kernels, staged(): pl.pallas_call(functools.partial(whole_kernel, depth, pieces), out_shape=...  129 us

profile of v3, /device:TPU:0, one launch (start us, length us, event | category | flops | bytes accessed | tf_op | source)
XLA Modules:
  0.0 137.4 jit_solution(3301023802129544075)
XLA Ops:
  0.0 0.7 stack.12
  0.7 0.7 stack.13
  1.5 0.7 stack.14
  2.2 0.7 pad_maximum_fusion.gains
  2.9 1.4 %reshape.6.own_clean = bf16[16,1152]{1,0:T(8,128)(2,1)} reshape(bf16[4,4608]{1,0:T(4,128)(2,1)} %param.14) | data formatting | bytes 73728 | tf_op jit(solution)/shard_map/reshape | solution.py:550
  4.3 1.4 %reshape.7.own_corrupt = bf16[16,1152]{1,0:T(8,128)(2,1)} reshape(bf16[4,4608]{1,0:T(4,128)(2,1)} %param.15) | data formatting | bytes 73728 | tf_op jit(solution)/shard_map/reshape | solution.py:550
  5.7 1.4 %copy.15.answers = s32[128,2]{1,0:T(8,128)} copy(s32[128,2]{0,1:T(2,128)} %param.16) | data formatting | bytes 2048 | tf_op args[2]
  7.1 129.0 %shard_map.136 = f32[1,2048]{1,0:T(1,128)} custom-call(bf16[16,1152]{1,0:T(8,128)(2,1)} %reshape.6.own_clean, bf16[16,1152]{1,0:T(8,128)(2,1)} %reshape.7.own_corrupt, s32[128,1]{1,0:T(8,128)} %constant.2.clone.target, s32[128,2]{1,0:T(8,128)} %copy.15.answers, f32[3,4608]{1,0:T(4,128)} %pad_maximum_fusion.gains, f32[1,2048]{1,0:T(1,128)} %bitcast.1, ...), custom_call_target="tpu_custom_call" | custom-call | tf_op jit(solution)/shard_map/pallas_call | solution.py:540
  136.1 1.3 copy.17
